TPU v7x, 512 devices: a whole 4x4x16 slice. The times are simulated.
512 devices in a mesh: dp: 16 (over y, z_hi), seq: 32 (over z_lo, x, core).
Axes of the slice: x: 4, y: 4, z: 16 (z_hi: 4, z_lo: 4; z = z_hi * 4 + z_lo), core: 2. Of those that a mesh axis runs over, the one named last changes fastest.
Arguments:
- tokens: bfloat16 [1024, 64, 1152], P(('dp', 'seq')), may hold values from -6 to 6
- spatial_qkv: bfloat16 [1024, 64, 1728], P(('dp', 'seq')), may hold values from -6 to 6
- wo_spatial: bfloat16 [576, 1152], replicated, may hold values from -0.25 to 0.25
- w_temporal: bfloat16 [1152, 1728], P(None, 'dp'), may hold values from -0.1875 to 0.1875
- wo_temporal: bfloat16 [576, 1152], replicated, may hold values from -0.25 to 0.25
- cotangent: bfloat16 [1024, 64, 1152], P(('dp', 'seq')), may hold values from -24 to 24
Outputs:
- block_out: bfloat16 [1024, 64, 1152], P(('dp', 'seq'))
- tokens_grad: bfloat16 [1024, 64, 1152], P(('dp', 'seq'))
- spatial_qkv_grad: bfloat16 [1024, 64, 1728], P(('dp', 'seq'))
- wo_spatial_grad: float32 [576, 1152], P('seq', 'dp')
- wo_temporal_grad: float32 [576, 1152], P('seq', 'dp')
All inputs are finite; a program needn't handle non-finite values.
Results may differ from a plain program's by a relative error of at most 0.038.
Values may be sent and summed in bfloat16 or wider, within the bound.
A program may use at most 64 MiB of HBM per device.

v0:
```python
import math
import jax
import jax.numpy as jnp
from jax import lax
from jax.sharding import PartitionSpec as P

DH = 72
FRAMES = 16


def split_three(packed):
    inner_width = packed.shape[-1] // 3
    return (
        packed[..., :inner_width],
        packed[..., inner_width : 2 * inner_width],
        packed[..., 2 * inner_width :],
    )


def head_view(matrix):
    batch_size, length, inner_width = matrix.shape
    return matrix.reshape(batch_size, length, inner_width // DH, DH)


def attention_weights_of(query_heads, key_heads):
    scores = jnp.einsum(
        "blhd,bmhd->bhlm", query_heads, key_heads, preferred_element_type=jnp.float32
    ) * (1.0 / math.sqrt(DH))
    return jax.nn.softmax(scores, axis=-1)


def attention(queries, key_rows, values):
    batch_size, length, inner_width = queries.shape
    weights_full = attention_weights_of(head_view(queries), head_view(key_rows))
    rounded = weights_full.astype(jnp.bfloat16)
    output = jnp.einsum(
        "bhlm,bmhd->blhd", rounded, head_view(values), preferred_element_type=jnp.float32
    )
    return output.reshape(batch_size, length, inner_width).astype(jnp.bfloat16)


def attention_grad(queries, key_rows, values, output_grad):
    batch_size, length, inner_width = queries.shape
    query_heads = head_view(queries)
    key_heads = head_view(key_rows)
    value_heads = head_view(values)
    grad_heads = head_view(output_grad)
    weights_full = attention_weights_of(query_heads, key_heads)
    rounded = weights_full.astype(jnp.bfloat16)
    value_grad = jnp.einsum(
        "bhlm,blhd->bmhd", rounded, grad_heads, preferred_element_type=jnp.float32
    )
    weight_grad = jnp.einsum(
        "blhd,bmhd->bhlm", grad_heads, value_heads, preferred_element_type=jnp.float32
    )
    centered = weight_grad - jnp.sum(weights_full * weight_grad, axis=-1, keepdims=True)
    score_grad = (weights_full * centered * (1.0 / math.sqrt(DH))).astype(jnp.bfloat16)
    query_grad = jnp.einsum(
        "bhlm,bmhd->blhd", score_grad, key_heads, preferred_element_type=jnp.float32
    )
    key_grad = jnp.einsum(
        "bhlm,blhd->bmhd", score_grad, query_heads, preferred_element_type=jnp.float32
    )
    joined = [
        part_grad.reshape(batch_size, length, inner_width)
        for part_grad in (query_grad, key_grad, value_grad)
    ]
    return jnp.concatenate(joined, axis=-1).astype(jnp.bfloat16)


def to_clips(matrix, clip_count):
    frame_total, patch_share, channels = matrix.shape
    grouped = matrix.reshape(clip_count, FRAMES, patch_share, channels).transpose(0, 2, 1, 3)
    return grouped.reshape(clip_count * patch_share, FRAMES, channels)


def from_clips(matrix, clip_count):
    batch_rows, frame_count, channels = matrix.shape
    patch_share = batch_rows // clip_count
    grouped = matrix.reshape(clip_count, patch_share, frame_count, channels).transpose(0, 2, 1, 3)
    return grouped.reshape(clip_count * frame_count, patch_share, channels)


def times_transposed(left, right):
    return lax.dot_general(
        left, right, (((1,), (1,)), ((), ())), preferred_element_type=jnp.float32
    )


def transposed_times(left, right):
    return lax.dot_general(
        left, right, (((0,), (0,)), ((), ())), preferred_element_type=jnp.float32
    )


def forward_project(hidden_rows, weight_shard):
    return jnp.dot(
        hidden_rows,
        lax.all_gather(weight_shard, "dp", axis=1, tiled=True),
        preferred_element_type=jnp.float32,
    )


def backward_project(grad_rows, weight_shard):
    return times_transposed(grad_rows, lax.all_gather(weight_shard, "dp", axis=1, tiled=True))


def shards(tokens, spatial_qkv, wo_spatial, w_temporal, wo_temporal, cotangent):
    frames_dev, patches, feature_width = tokens.shape
    row_total = frames_dev * patches
    seq_devices = lax.axis_size("seq")
    clip_count = frames_dev * seq_devices // FRAMES
    spatial_query, spatial_keys, spatial_values = split_three(spatial_qkv)
    spatial_out = attention(spatial_query, spatial_keys, spatial_values)
    spatial_rows = spatial_out.reshape(row_total, -1)
    hidden_rows = (
        tokens.reshape(row_total, feature_width).astype(jnp.float32)
        + jnp.dot(spatial_rows, wo_spatial, preferred_element_type=jnp.float32)
    ).astype(jnp.bfloat16)
    frame_qkv = (
        forward_project(hidden_rows, w_temporal)
        .astype(jnp.bfloat16)
        .reshape(frames_dev, patches, -1)
    )
    patch_qkv = lax.all_to_all(frame_qkv, "seq", split_axis=1, concat_axis=0, tiled=True)
    temporal_query, temporal_keys, temporal_values = split_three(to_clips(patch_qkv, clip_count))
    patch_out = from_clips(attention(temporal_query, temporal_keys, temporal_values), clip_count)
    temporal_out = lax.all_to_all(patch_out, "seq", split_axis=0, concat_axis=1, tiled=True)
    temporal_rows = temporal_out.reshape(row_total, -1)
    block_out = (
        hidden_rows.astype(jnp.float32)
        + jnp.dot(temporal_rows, wo_temporal, preferred_element_type=jnp.float32)
    ).astype(jnp.bfloat16)
    grad_rows = cotangent.reshape(row_total, feature_width)
    out_grad = (
        times_transposed(grad_rows, wo_temporal)
        .astype(jnp.bfloat16)
        .reshape(frames_dev, patches, -1)
    )
    temporal_part = transposed_times(temporal_rows, grad_rows).astype(jnp.bfloat16)
    patch_out_grad = lax.all_to_all(out_grad, "seq", split_axis=1, concat_axis=0, tiled=True)
    clip_qkv_grad = attention_grad(
        temporal_query, temporal_keys, temporal_values, to_clips(patch_out_grad, clip_count)
    )
    patch_qkv_grad = from_clips(clip_qkv_grad, clip_count)
    frame_qkv_grad = lax.all_to_all(patch_qkv_grad, "seq", split_axis=0, concat_axis=1, tiled=True)
    projection_grad = backward_project(frame_qkv_grad.reshape(row_total, -1), w_temporal).astype(
        jnp.bfloat16
    )
    tokens_grad = (grad_rows.astype(jnp.float32) + projection_grad.astype(jnp.float32)).astype(
        jnp.bfloat16
    )
    spatial_out_grad = (
        times_transposed(tokens_grad, wo_spatial)
        .astype(jnp.bfloat16)
        .reshape(frames_dev, patches, -1)
    )
    spatial_part = transposed_times(spatial_rows, tokens_grad).astype(jnp.bfloat16)
    spatial_qkv_grad = attention_grad(spatial_query, spatial_keys, spatial_values, spatial_out_grad)
    seq_sums = (
        lax.psum_scatter(spatial_part, "seq", scatter_dimension=0, tiled=True).astype(jnp.float32),
        lax.psum_scatter(temporal_part, "seq", scatter_dimension=0, tiled=True).astype(jnp.float32),
    )
    spatial_weight_grad, temporal_weight_grad = (
        lax.psum_scatter(
            seq_sums[0].astype(jnp.bfloat16), "dp", scatter_dimension=1, tiled=True
        ).astype(jnp.float32),
        lax.psum_scatter(
            seq_sums[1].astype(jnp.bfloat16), "dp", scatter_dimension=1, tiled=True
        ).astype(jnp.float32),
    )
    return (
        block_out.reshape(frames_dev, patches, feature_width),
        tokens_grad.reshape(frames_dev, patches, feature_width),
        spatial_qkv_grad,
        spatial_weight_grad,
        temporal_weight_grad,
    )


def solution(mesh):
    placed = (
        P(("dp", "seq"), None, None),
        P(("dp", "seq"), None, None),
        P(),
        P(None, "dp"),
        P(),
        P(("dp", "seq"), None, None),
    )
    return jax.shard_map(
        shards,
        mesh=mesh,
        in_specs=placed,
        out_specs=(
            P(("dp", "seq"), None, None),
            P(("dp", "seq"), None, None),
            P(("dp", "seq"), None, None),
            P("seq", "dp"),
            P("seq", "dp"),
        ),
        check_vma=False,
    )
```

profile of v0, /device:TPU:2, one launch (start us, length us, event | category | flops | bytes accessed | tf_op | source)
XLA Modules:
  0.0 741.1 jit_solution(11731465842137330203)
XLA Ops:
  8.5 1.5 convolution_convert_fusion.13
  11.0 10.1 %all-to-all-start.2 = ((bf16[2,64,576]{2,0,1:T(2,128)(2,1)}), bf16[2,64,576]{2,0,1:T(2,128)(2,1)}, u32[]{:S(2)}, u32[]{:S(2)}) async-start(bf16[2,64,576]{2,0,1:T(2,128)(2,1)} %copy.76), calls=%async_computation.2 | async-start | bytes 327680 | tf_op jit(solution)/shard_map/all_to_all | solution.py:141
  22.1 1.2 fusion.123
  23.3 2.4 fusion.21
  25.7 1.1 copy.62
  27.4 121.9 %all-gather.3.cloned.1.call-done = bf16[16,108,1152]{2,1,0:T(8,128)(2,1)} async-done(((bf16[1,108,1152]{2,1,0:T(8,128)(2,1)}), bf16[16,108,1152]{2,1,0:T(8,128)(2,1)}) %all-gather.3.cloned.1.call-update) | async-done | bytes 3981328 | tf_op jit(solution)/shard_map/all_gather | solution.py:99
  149.4 4.8 reshape.139
  154.2 4.1 convolution_convert_fusion.3
  158.3 1.2 copy.63
  159.5 1.2 copy.64
  160.8 5.0 all-to-all-start
  165.7 1.0 copy.77
  167.5 1.9 reshape_reshape.6
  169.4 9.7 %all-to-all-done = bf16[2,64,1728]{2,0,1:T(2,128)(2,1)S(1)} async-done(((bf16[2,64,1728]{2,0,1:T(2,128)(2,1)}), bf16[2,64,1728]{2,0,1:T(2,128)(2,1)S(1)}, u32[]{:S(2)}, u32[]{:S(2)}) %all-to-all-start) | async-done | bytes 442400 | tf_op jit(solution)/shard_map/all_to_all | solution.py:125
  180.2 1.9 reshape.123
  182.1 1.0 reshape.124
  183.1 1.2 reshape.122
  184.3 1.1 fusion.42
  185.4 2.2 fusion.128
  187.6 2.3 fusion.22
  189.9 1.0 copy.71
  193.5 5.9 all-to-all-start.1
  199.4 2.2 fusion.25
  201.6 1.0 copy.87
  203.5 1.9 fusion.24
  206.3 2.0 fusion.23
  209.3 1.2 concatenate.18
  210.6 1.2 copy.89
  211.8 8.0 %all-to-all-start.3 = ((bf16[64,2,1728]{2,1,0:T(2,128)(2,1)}), bf16[64,2,1728]{2,1,0:T(2,128)(2,1)}, u32[]{:S(2)}, u32[]{:S(2)}) async-start(bf16[64,2,1728]{2,1,0:T(2,128)(2,1)} %copy.89), calls=%async_computation.3 | async-start | bytes 917504 | tf_op jit(solution)/shard_map/all_to_all | solution.py:146
  219.8 1.7 copy.198
  221.5 1.0 reshape.126
  222.6 1.6 convolution_convert_fusion
  224.2 8.9 %all-to-all-done.3 = bf16[64,2,1728]{2,1,0:T(2,128)(2,1)} async-done(((bf16[64,2,1728]{2,1,0:T(2,128)(2,1)}), bf16[64,2,1728]{2,1,0:T(2,128)(2,1)}, u32[]{:S(2)}, u32[]{:S(2)}) %all-to-all-start.3) | async-done | bytes 442400 | tf_op jit(solution)/shard_map/all_to_all | solution.py:146
  233.1 2.1 copy.197
  235.2 2.2 reshape.132
  237.4 3.1 fusion.6
  240.5 1.6 convolution_convert_fusion.1
  242.2 1.3 dynamic-slice.2
  243.5 1.3 dynamic-slice
  246.1 1.1 fusion.8
  248.7 1.7 fusion.26
  250.8 275.0 %all-reduce.9.cloned.1.call-done = (bf16[576,1152]{1,0:T(8,128)(2,1)}, bf16[576,1152]{1,0:T(8,128)(2,1)}) async-done(((bf16[576,1152]{1,0:T(8,128)(2,1)}, bf16[576,1152]{1,0:T(8,128)(2,1)}), (bf16[576,1152]{1,0:T(8,128)(2,1)}, bf16[576,1152]{1,0:T(8,128)(2,1)})) %all-reduce.9.cloned.1.call-update) | async-done | bytes 2654224
  525.8 1.6 constant_dynamic-slice_fusion
  527.4 1.6 fusion.27
  530.2 1.0 concatenate.19
  531.1 200.7 %all-reduce.11.cloned.1.call-done = (bf16[18,1152]{1,0:T(8,128)(2,1)}, bf16[18,1152]{1,0:T(8,128)(2,1)}) async-done(((bf16[18,1152]{1,0:T(8,128)(2,1)}, bf16[18,1152]{1,0:T(8,128)(2,1)}), (bf16[18,1152]{1,0:T(8,128)(2,1)}, bf16[18,1152]{1,0:T(8,128)(2,1)})) %all-reduce.11.cloned.1.call-update) | async-done | bytes 82960
  731.8 1.4 dynamic-slice_convert_fusion.1
  733.2 1.4 dynamic-slice_convert_fusion
  (74 shorter events, 14.2 us)
Async XLA Ops:
  7.2 1.3 copy-start
  7.2 142.2 %all-gather.3.cloned.1.call-start = ((), (), s32[]{:S(2)}) async-start(), calls=%async_computation.4 | async-start | bytes 4386816 | tf_op jit(solution)/shard_map/all_gather | solution.py:99
  8.5 12.6 %copy-start.11 = (bf16[2,64,1728]{2,1,0:T(8,128)(2,1)S(1)}, bf16[2,64,1728]{2,1,0:T(8,128)(2,1)}, u32[]{:S(2)}) copy-start(bf16[2,64,1728]{2,1,0:T(8,128)(2,1)} %param.7) | copy-start | bytes 1327108
  11.0 149.7 %all-to-all-start.2 = ((bf16[2,64,576]{2,0,1:T(2,128)(2,1)}), bf16[2,64,576]{2,0,1:T(2,128)(2,1)}, u32[]{:S(2)}, u32[]{:S(2)}) async-start(bf16[2,64,576]{2,0,1:T(2,128)(2,1)} %copy.76), calls=%async_computation.2 | async-start | bytes 327680 | tf_op jit(solution)/shard_map/all_to_all | solution.py:141
  21.5 1.8 copy-start.13
  21.8 1.5 copy-start.15
  22.1 1.2 copy-start.8
  23.3 3.7 copy-start.1
  23.3 3.7 copy-start.12
  27.0 127.2 %copy-start.4 = (bf16[128,576]{1,0:T(8,128)(2,1)}, bf16[128,576]{1,0:T(8,128)(2,1)S(1)}, u32[]{:S(2)}) copy-start(bf16[128,576]{1,0:T(8,128)(2,1)S(1)} %convert_element_type.94) | copy-start | bytes 442372
  160.8 18.3 %all-to-all-start = ((bf16[2,64,1728]{2,0,1:T(2,128)(2,1)}), bf16[2,64,1728]{2,0,1:T(2,128)(2,1)S(1)}, u32[]{:S(2)}, u32[]{:S(2)}) async-start(bf16[2,64,1728]{2,0,1:T(2,128)(2,1)} %copy.64), calls=%async_computation | async-start | bytes 917504 | tf_op jit(solution)/shard_map/all_to_all | solution.py:125
  179.5 4.9 copy-start.10
  193.5 18.3 %all-to-all-start.1 = ((bf16[64,2,576]{2,1,0:T(2,128)(2,1)}), bf16[64,2,576]{2,1,0:T(2,128)(2,1)}, u32[]{:S(2)}, u32[]{:S(2)}) async-start(bf16[64,2,576]{2,1,0:T(2,128)(2,1)} %copy.73), calls=%async_computation.1 | async-start | bytes 327680 | tf_op jit(solution)/shard_map/all_to_all | solution.py:128
  210.6 12.0 %copy-start.2 = (bf16[2,64,1152]{2,1,0:T(8,128)(2,1)S(1)}, bf16[2,64,1152]{2,1,0:T(8,128)(2,1)}, u32[]{:S(2)}) copy-start(bf16[2,64,1152]{2,1,0:T(8,128)(2,1)} %param.11) | copy-start | bytes 884740
  211.8 21.3 %all-to-all-start.3 = ((bf16[64,2,1728]{2,1,0:T(2,128)(2,1)}), bf16[64,2,1728]{2,1,0:T(2,128)(2,1)}, u32[]{:S(2)}, u32[]{:S(2)}) async-start(bf16[64,2,1728]{2,1,0:T(2,128)(2,1)} %copy.89), calls=%async_computation.3 | async-start | bytes 917504 | tf_op jit(solution)/shard_map/all_to_all | solution.py:146
  219.8 306.0 %all-reduce.9.cloned.1.call-start = ((), (), s32[]{:S(2)}) async-start(), calls=%async_computation.5 | async-start | bytes 5308416
  222.6 12.7 %copy-start.6 = (bf16[128,576]{1,0:T(8,128)(2,1)}, bf16[128,576]{1,0:T(8,128)(2,1)S(1)}, u32[]{:S(2)}) copy-start(bf16[128,576]{1,0:T(8,128)(2,1)S(1)} %reshape.126) | copy-start | bytes 442372
  237.4 3.1 copy-start.5
  240.5 6.7 copy-start.3
  242.1 3.9 copy-start.7
  242.2 489.6 %all-reduce.11.cloned.1.call-start = ((), (), s32[]{:S(2)}) async-start(), calls=%async_computation.6 | async-start | bytes 221184
  247.2 1.0 copy-start.9
  247.7 1.0 copy-start.16
  248.7 1.7 copy-start.14
Sparse Core Ops, SparseCore 0:
  11.1 138.2 all-gather.2
  242.3 283.4 all-reduce.8
  528.8 202.9 all-reduce.10
where the time goes:
time: 742 us; the launch traced here: 741 us
  waiting for transfers between devices  617 us (83%)
  local copies, waits for them, and re-layouts  43.8 us (6%)
  matrix products  33.1 us (4%)
  starting transfers between devices  29 us (4%)
  between operations  15.5 us (2%)
    unnamed x5, waiting for transfers between devices  476 us
    all_gather x1, waiting for transfers between devices, forward_project(): lax.all_gather(weight_shard, 'dp', axis=1, tiled=True)  122 us
  transfers between devices with their start and end apart: 7, of which 5 were waited for; matrix products, arithmetic and copies ran while one was open for 7% of the time, Pallas kernels for 0%

commit v1 on v0

--- a/solution.py
+++ b/solution.py
@@ -143,7 +143,19 @@
         temporal_query, temporal_keys, temporal_values, to_clips(patch_out_grad, clip_count)
     )
     patch_qkv_grad = from_clips(clip_qkv_grad, clip_count)
-    frame_qkv_grad = lax.all_to_all(patch_qkv_grad, "seq", split_axis=0, concat_axis=1, tiled=True)
+
+    def part_state(a0, chip_axis, dimension_no, axis_k):
+        return jnp.concatenate(
+            lax.all_to_all(
+                jnp.stack(jnp.split(a0, lax.axis_size(chip_axis), dimension_no), axis=0),
+                chip_axis,
+                0,
+                0,
+            ),
+            axis=axis_k,
+        )
+
+    frame_qkv_grad = part_state(patch_qkv_grad, "seq", 0, 1)
     projection_grad = backward_project(frame_qkv_grad.reshape(row_total, -1), w_temporal).astype(
         jnp.bfloat16
     )

time: 742 us -> 789 us (1.063)
  local copies, waits for them, and re-layouts: 43.8 us -> 86.8 us
    unnamed x38 -> x73, local copies, waits for them, and re-layouts: 9.97 us -> 54.5 us
  transfers between devices with their start and end apart: 7 -> 7, of which waited for: 5 -> 5; matrix products, arithmetic and copies ran while one was open for 7% -> 11% of each run, Pallas kernels for 0% -> 0%
where the time goes in v1:
time: 789 us; the launch traced here: 786 us
  waiting for transfers between devices  618 us (78%)
  local copies, waits for them, and re-layouts  86.8 us (11%)
  matrix products  34.2 us (4%)
  starting transfers between devices  28.8 us (4%)
  between operations  15.5 us (2%)
    unnamed x5, waiting for transfers between devices  476 us
    all_gather x1, waiting for transfers between devices, forward_project(): lax.all_gather(weight_shard, 'dp', axis=1, tiled=True)  122 us
    unnamed x73, local copies, waits for them, and re-layouts  54.5 us
  transfers between devices with their start and end apart: 7, of which 5 were waited for; matrix products, arithmetic and copies ran while one was open for 11% of the time, Pallas kernels for 0%

profile of v1, /device:TPU:2, one launch (start us, length us, event | category | flops | bytes accessed | tf_op | source)
XLA Modules:
  0.0 785.9 jit_solution(7941023724379906741)
XLA Ops:
  8.5 1.5 convolution_convert_fusion.13
  11.0 10.1 %all-to-all-start.2 = ((bf16[2,64,576]{2,0,1:T(2,128)(2,1)}), bf16[2,64,576]{2,0,1:T(2,128)(2,1)}, u32[]{:S(2)}, u32[]{:S(2)}) async-start(bf16[2,64,576]{2,0,1:T(2,128)(2,1)} %copy.76), calls=%async_computation.2 | async-start | bytes 327680 | tf_op jit(solution)/shard_map/all_to_all | solution.py:141
  23.3 2.4 fusion.21
  27.4 122.0 %all-gather.3.cloned.1.call-done = bf16[16,108,1152]{2,1,0:T(8,128)(2,1)} async-done(((bf16[1,108,1152]{2,1,0:T(8,128)(2,1)}), bf16[16,108,1152]{2,1,0:T(8,128)(2,1)}) %all-gather.3.cloned.1.call-update) | async-done | bytes 3981328 | tf_op jit(solution)/shard_map/all_gather | solution.py:99
  149.4 4.9 reshape.138
  154.2 4.1 convolution_convert_fusion.3
  160.8 5.0 all-to-all-start
  167.5 1.9 reshape_reshape.9
  169.4 9.7 %all-to-all-done = bf16[2,64,1728]{2,0,1:T(2,128)(2,1)S(1)} async-done(((bf16[2,64,1728]{2,0,1:T(2,128)(2,1)}), bf16[2,64,1728]{2,0,1:T(2,128)(2,1)S(1)}, u32[]{:S(2)}, u32[]{:S(2)}) %all-to-all-start) | async-done | bytes 442400 | tf_op jit(solution)/shard_map/all_to_all | solution.py:125
  184.4 2.2 fusion.128
  186.6 2.2 fusion.25
  188.8 2.3 fusion.22
  191.1 2.8 fusion.23
  193.9 2.3 fusion.24
  205.1 5.9 all-to-all-start.1
  211.0 1.5 constant_dynamic-update-slice_fusion.31
  212.4 1.4 constant_dynamic-update-slice_fusion.30
  213.9 1.4 constant_dynamic-update-slice_fusion.29
  215.3 1.4 constant_dynamic-update-slice_fusion.28
  218.2 1.4 constant_dynamic-update-slice_fusion.26
  219.6 1.4 constant_dynamic-update-slice_fusion.25
  221.0 1.4 constant_dynamic-update-slice_fusion.24
  223.9 1.4 constant_dynamic-update-slice_fusion.22
  225.3 1.4 constant_dynamic-update-slice_fusion.21
  226.8 1.4 constant_dynamic-update-slice_fusion.20
  231.1 1.4 constant_dynamic-update-slice_fusion.17
  232.5 1.4 constant_dynamic-update-slice_fusion.16
  233.9 1.4 constant_dynamic-update-slice_fusion.15
  236.8 1.4 constant_dynamic-update-slice_fusion.13
  238.2 1.4 constant_dynamic-update-slice_fusion.12
  241.1 1.5 constant_dynamic-update-slice_fusion.10
  244.0 1.4 constant_dynamic-update-slice_fusion.8
  248.3 1.4 constant_dynamic-update-slice_fusion.5
  249.7 1.4 constant_dynamic-update-slice_fusion.4
  254.0 1.4 constant_dynamic-update-slice_fusion.1
  255.4 1.4 constant_dynamic-update-slice_fusion
  256.9 7.8 all-to-all-start.3
  266.6 1.6 convolution_convert_fusion
  268.2 9.8 %all-to-all-done.3 = bf16[32,2,2,1728]{3,1,2,0:T(2,128)(2,1)} async-done(((bf16[32,2,2,1728]{3,1,2,0:T(2,128)(2,1)}), bf16[32,2,2,1728]{3,1,2,0:T(2,128)(2,1)}, u32[]{:S(2)}, u32[]{:S(2)}) %all-to-all-start.3) | async-done | bytes 442400 | tf_op jit(solution)/shard_map/all_to_all | solution.py:149
  278.0 2.1 copy.89
  280.2 2.1 reshape_reshape.10
  282.3 3.1 fusion.6
  285.4 1.6 convolution_convert_fusion.1
  293.5 1.7 fusion.26
  295.6 275.0 %all-reduce.9.cloned.1.call-done = (bf16[576,1152]{1,0:T(8,128)(2,1)}, bf16[576,1152]{1,0:T(8,128)(2,1)}) async-done(((bf16[576,1152]{1,0:T(8,128)(2,1)}, bf16[576,1152]{1,0:T(8,128)(2,1)}), (bf16[576,1152]{1,0:T(8,128)(2,1)}, bf16[576,1152]{1,0:T(8,128)(2,1)})) %all-reduce.9.cloned.1.call-update) | async-done | bytes 2654224
  570.6 1.6 constant_dynamic-slice_fusion
  572.2 1.6 fusion.27
  576.0 200.7 %all-reduce.11.cloned.1.call-done = (bf16[18,1152]{1,0:T(8,128)(2,1)}, bf16[18,1152]{1,0:T(8,128)(2,1)}) async-done(((bf16[18,1152]{1,0:T(8,128)(2,1)}, bf16[18,1152]{1,0:T(8,128)(2,1)}), (bf16[18,1152]{1,0:T(8,128)(2,1)}, bf16[18,1152]{1,0:T(8,128)(2,1)})) %all-reduce.11.cloned.1.call-update) | async-done | bytes 82960
  (109 shorter events, 52.5 us)
Async XLA Ops:
  7.2 1.3 copy-start
  7.2 142.2 %all-gather.3.cloned.1.call-start = ((), (), s32[]{:S(2)}) async-start(), calls=%async_computation.4 | async-start | bytes 4386816 | tf_op jit(solution)/shard_map/all_gather | solution.py:99
  8.5 12.6 %copy-start.11 = (bf16[2,64,1728]{2,1,0:T(8,128)(2,1)S(1)}, bf16[2,64,1728]{2,1,0:T(8,128)(2,1)}, u32[]{:S(2)}) copy-start(bf16[2,64,1728]{2,1,0:T(8,128)(2,1)} %param.7) | copy-start | bytes 1327108
  11.0 149.8 %all-to-all-start.2 = ((bf16[2,64,576]{2,0,1:T(2,128)(2,1)}), bf16[2,64,576]{2,0,1:T(2,128)(2,1)}, u32[]{:S(2)}, u32[]{:S(2)}) async-start(bf16[2,64,576]{2,0,1:T(2,128)(2,1)} %copy.76), calls=%async_computation.2 | async-start | bytes 327680 | tf_op jit(solution)/shard_map/all_to_all | solution.py:141
  21.5 1.8 copy-start.15
  21.8 1.5 copy-start.17
  22.1 1.2 copy-start.8
  23.3 3.7 copy-start.1
  23.3 3.7 copy-start.13
  27.0 127.3 %copy-start.4 = (bf16[128,576]{1,0:T(8,128)(2,1)}, bf16[128,576]{1,0:T(8,128)(2,1)S(1)}, u32[]{:S(2)}) copy-start(bf16[128,576]{1,0:T(8,128)(2,1)S(1)} %convert_element_type.94) | copy-start | bytes 442372
  160.8 18.3 %all-to-all-start = ((bf16[2,64,1728]{2,0,1:T(2,128)(2,1)}), bf16[2,64,1728]{2,0,1:T(2,128)(2,1)S(1)}, u32[]{:S(2)}, u32[]{:S(2)}) async-start(bf16[2,64,1728]{2,0,1:T(2,128)(2,1)} %copy.64), calls=%async_computation | async-start | bytes 917504 | tf_op jit(solution)/shard_map/all_to_all | solution.py:125
  179.5 3.9 copy-start.10
  191.1 2.8 copy-start.12
  196.2 3.8 copy-start.14
  205.1 51.8 %all-to-all-start.1 = ((bf16[64,2,576]{2,1,0:T(2,128)(2,1)}), bf16[64,2,576]{2,1,0:T(2,128)(2,1)S(1)}, u32[]{:S(2)}, u32[]{:S(2)}) async-start(bf16[64,2,576]{2,1,0:T(2,128)(2,1)} %copy.73), calls=%async_computation.1 | async-start | bytes 327680 | tf_op jit(solution)/shard_map/all_to_all | solution.py:128
  210.9 55.6 %copy-start.2 = (bf16[2,64,1152]{2,1,0:T(8,128)(2,1)S(1)}, bf16[2,64,1152]{2,1,0:T(8,128)(2,1)}, u32[]{:S(2)}) copy-start(bf16[2,64,1152]{2,1,0:T(8,128)(2,1)} %param.11) | copy-start | bytes 884740
  256.9 21.1 %all-to-all-start.3 = ((bf16[32,2,2,1728]{3,1,2,0:T(2,128)(2,1)}), bf16[32,2,2,1728]{3,1,2,0:T(2,128)(2,1)}, u32[]{:S(2)}, u32[]{:S(2)}) async-start(bf16[32,2,2,1728]{3,1,2,0:T(2,128)(2,1)} %constant_dynamic-update-slice_fusion), calls=%async_computation.3 | async-start | bytes 917504 | tf_op jit(solution)/shard_map/all_to_all | solution.py:149
  264.7 306.0 %all-reduce.9.cloned.1.call-start = ((), (), s32[]{:S(2)}) async-start(), calls=%async_computation.5 | async-start | bytes 5308416
  266.5 13.6 %copy-start.6 = (bf16[128,576]{1,0:T(8,128)(2,1)}, bf16[128,576]{1,0:T(8,128)(2,1)S(1)}, u32[]{:S(2)}) copy-start(bf16[128,576]{1,0:T(8,128)(2,1)S(1)} %reshape.125) | copy-start | bytes 442372
  282.3 3.1 copy-start.5
  285.4 6.7 copy-start.3
  287.0 3.9 copy-start.7
  287.0 489.6 %all-reduce.11.cloned.1.call-start = ((), (), s32[]{:S(2)}) async-start(), calls=%async_computation.6 | async-start | bytes 221184
  292.0 1.0 copy-start.9
  292.6 1.0 copy-start.18
  293.5 1.7 copy-start.16
Sparse Core Ops, SparseCore 0:
  11.1 138.2 all-gather.2
  287.1 283.4 all-reduce.8
  573.6 202.9 all-reduce.10
